TPU v7x, 32 devices: a whole 2x2x4 slice. The times are simulated.
32 devices in a mesh: outer: 4 (over z), inner: 8 (over y, x, core).
Axes of the slice: x: 2, y: 2, z: 4, core: 2. Of those that a mesh axis runs over, the one named last changes fastest.
Arguments:
- queries: bfloat16 [4096, 32, 128], P(('outer', 'inner')), may hold values from -8 to 8
- key_states: bfloat16 [4096, 4, 128], P(('outer', 'inner')), may hold values from -8 to 8
- value_states: bfloat16 [4096, 4, 128], P(('outer', 'inner')), may hold values from -6 to 6
- out_grad: bfloat16 [4096, 32, 128], P(('outer', 'inner')), may hold values from -6 to 6
- bounds: int32 [3, 4096], P(None, ('outer', 'inner')), may hold values from 0 to 4095, as said below
Outputs:
- query_grad: bfloat16 [4096, 32, 128], P(('outer', 'inner'))
- key_grad: bfloat16 [4096, 4, 128], P(('outer', 'inner'))
- value_grad: bfloat16 [4096, 4, 128], P(('outer', 'inner'))
Inputs may be any that keep to these rules, and one draw needn't show every extreme that they name: For each token t, bounds[0, t] is the first token of t's document (tokens of a document are consecutive), with t - 512 < bounds[0, t] <= t; in every draw some token has t - bounds[0, t] = 511. Either bounds[1, t] = bounds[2, t] = 0, or bounds[0, t] + 2 <= bounds[1, t] < bounds[2, t] <= t.
All inputs are finite; a program needn't handle non-finite values.
Results may differ from a plain program's by a relative error of at most 0.006.
Values may be sent and summed in bfloat16 or wider, within the bound.
No kernel may reach another device: no remote copies, remote signals or barrier semaphores. Data moves between devices by JAX's collectives and lax.ppermute only.
A program may use at most 64 MiB of HBM per device.

v0:
```python
import functools
import math

import jax
import jax.numpy as jnp
from jax import lax
from jax.experimental import pallas as pl
from jax.experimental.pallas import tpu as pltpu
from jax.sharding import PartitionSpec as P


AXES = ("outer", "inner")
SPAN = 4
HIDDEN = -1e30
VMEM = pl.BlockSpec(memory_space=pltpu.VMEM)
SMEM = pl.BlockSpec(memory_space=pltpu.SMEM)
HBM = pl.BlockSpec(memory_space=pltpu.HBM)
NT = (((1,), (1,)), ((), ()))
NN = (((1,), (0,)), ((), ()))
BF = jnp.bfloat16
F32 = jnp.float32
TILE = 64
WIDTH = 512
CHUNKS = 2


def rotated(shard, by):
    peers = lax.axis_size(AXES)
    return lax.ppermute(shard, AXES, [(i, (i + by) % peers) for i in range(peers)])


def rotated_pair(shards, way):
    far = rotated(shards[0], way * SPAN)
    near = rotated(shards[1], way * SPAN // 2)
    return far, near


def swapped(shard):
    peers = lax.axis_size(AXES)
    return lax.ppermute(shard, AXES, [(i, i ^ 1) for i in range(peers)])


def dot(a, b, dims):
    return lax.dot_general(a, b, dims, preferred_element_type=F32)


def in_hbm(x):
    return pltpu.with_memory_space_constraint(x, pltpu.HBM)


def call(body, outs, args, specs=None, scratch=(), flops=0, mib=16):
    return pl.pallas_call(
        body,
        out_shape=outs,
        in_specs=specs or [VMEM] * len(args),
        out_specs=jax.tree.map(lambda _: VMEM, outs),
        scratch_shapes=list(scratch),
        compiler_params=pltpu.CompilerParams(vmem_limit_bytes=mib << 20),
        cost_estimate=pl.CostEstimate(flops=flops, bytes_accessed=1 << 20, transcendentals=0),
    )(*args)


def fetch(sources, targets, sems):
    copies = [pltpu.make_async_copy(a, b, sems.at[i]) for i, (a, b) in enumerate(zip(sources, targets))]
    for copy in copies:
        copy.start()
    return copies


def pack_body(k_hbm, v_hbm, *refs):
    kv_refs, (raw_ref, wide_ref, sems) = refs[:-3], refs[-3:]
    part, rows, _ = kv_refs[0].shape
    part //= 2
    heads = part * CHUNKS
    copies = fetch((k_hbm, v_hbm), (raw_ref.at[0], raw_ref.at[1]), sems)
    for half in range(2):
        copies[half].wait()
        wide_ref[half] = raw_ref[half].astype(F32)
        for c in range(heads):
            kv_refs[c // part][half * part + c % part] = wide_ref[half, pl.ds(c, rows, stride=heads), :].astype(BF)


def prepare_body(me_ref, q_hbm, g_hbm, bounds_hbm, *refs):
    kv_refs, outs = refs[:CHUNKS], refs[CHUNKS:]
    qr_ref, gr_ref, bias_ref, outside_ref, sides_ref, s_ref, w_ref, q_ref, g_ref, bounds_ref, inside_ref, sems = outs
    first, *copies = fetch((bounds_hbm, q_hbm, g_hbm), (bounds_ref, q_ref, g_ref), sems)
    first.wait()
    rows, heads, depth = q_ref.shape
    kv_heads = qr_ref.shape[0]
    part = kv_heads // CHUNKS
    group = heads // kv_heads
    lanes = rows * group
    local = lax.broadcasted_iota(jnp.int32, (rows, rows), 0)
    token = lax.broadcasted_iota(jnp.int32, (rows, rows), 1)
    wide_token = lax.broadcasted_iota(jnp.int32, (rows, lanes), 0)
    wide_lane = lax.broadcasted_iota(jnp.int32, (rows, lanes), 1)
    widen = (wide_lane // group == wide_token).astype(BF)
    me = me_ref[0]
    odd = lax.rem(me, 2)
    start = bounds_ref[0:1, :] - me * rows
    low = bounds_ref[1:2, :] - me * rows
    high = bounds_ref[2:3, :] - me * rows
    x_offset = 1 + 2 * odd

    key_any = local >= 0

    def hidden(offset, also):
        key = local - offset * rows
        seen = (key >= start) & ((key < low) | (key >= high)) & also
        return dot(jnp.where(seen, 0.0, HIDDEN).astype(BF), widen, NN)

    inside = local <= token
    inside_ref[0] = hidden(0, inside)
    for at, offset in enumerate((SPAN, 2, x_offset, SPAN - x_offset)):
        bias_ref[at * rows : (at + 1) * rows, :] = hidden(offset, ~inside if at == 0 else key_any)
    wide = dot(inside.astype(F32).astype(BF), widen, NN)
    inside_ref[1] = wide
    sides_ref[0] = wide.astype(BF)
    wide = 1.0 - wide
    outside_ref[...] = wide
    sides_ref[1] = wide.astype(BF)
    for copy in copies:
        copy.wait()
    for c in range(kv_heads):
        own = slice(c * group, (c + 1) * group)
        qr_ref[c] = q_ref[:, own, :].astype(F32).reshape(lanes, depth).astype(BF)
        gr_ref[c] = g_ref[:, own, :].astype(F32).reshape(lanes, depth).astype(BF)
        s_ref[c] = dot(kv_refs[c // part][c % part], qr_ref[c], NT) + inside_ref[0]
        w_ref[c] = dot(kv_refs[c // part][part + c % part], gr_ref[c], NT) * inside_ref[1]


def lanes_of(far_ref, near_ref, pair_ref):
    half = pair_ref.shape[0] // 2
    return far_ref, near_ref, pair_ref.at[:half], pair_ref.at[half:]


def key_value_grads(ds_ref, p_ref, q_ref, g_ref, out_refs, c):
    part, rows, _ = out_refs[0].shape
    dk = dot(ds_ref[...], q_ref[...], NN).astype(BF)
    dv = dot(p_ref[...], g_ref[...], NN).astype(BF)
    for i, ref in enumerate(out_refs):
        ref[c] = dk[i * rows : (i + 1) * rows]
        ref[part // 2 + c] = dv[i * rows : (i + 1) * rows]


def main_body(first, *refs):
    kv_refs = lanes_of(*refs[:3])
    qr_ref, gr_ref, bias_ref, outside_ref, sides_ref, s_ref, w_ref = refs[3:10]
    pair_ref, ds_ref, p_ref, rest_ref, k_all, v_all, p_all = refs[10:]
    _, lanes, depth = qr_ref.shape
    kv_heads = kv_refs[0].shape[0] // 2
    rows = s_ref.shape[1]
    far = SPAN * rows
    scale = depth ** -0.5
    rate = scale * math.log2(math.e)
    chunks = lanes // WIDTH
    fold = lambda x: x.reshape(TILE // 8, 8, WIDTH)
    tiles = [slice(r, r + TILE) for r in range(0, far, TILE)]

    def chunk(c, n):
        cols = slice(n * WIDTH, (n + 1) * WIDTH)
        s = dot(k_all[...], qr_ref[first + c, cols, :], NT)
        w = dot(v_all[...], gr_ref[first + c, cols, :], NT)
        top = jnp.full((8, WIDTH), HIDDEN, F32)
        scores, weighs, raws = [], [], []
        for at in tiles:
            s_tile = s[at] + bias_ref[at, cols]
            w_tile = w[at]
            if at.start < rows:
                s_tile = jnp.maximum(s_tile, s_ref[first + c, at, cols])
                w_tile = w_tile * outside_ref[at, cols] + w_ref[first + c, at, cols]
            scores.append(s_tile)
            weighs.append(w_tile)
            top = jnp.maximum(top, jnp.max(fold(s_tile), axis=0))
        top = jnp.max(top, axis=0, keepdims=True)
        total = jnp.zeros((8, WIDTH), F32)
        delta = jnp.zeros((8, WIDTH), F32)
        for s_tile, w_tile in zip(scores, weighs):
            e = jnp.exp2((s_tile - top) * rate)
            raws.append(e)
            total = total + jnp.sum(fold(e), axis=0)
            delta = delta + jnp.sum(fold(e * w_tile), axis=0)
        inverse = 1.0 / jnp.sum(total, axis=0, keepdims=True)
        delta = jnp.sum(delta, axis=0, keepdims=True) * inverse
        for at, e, w_tile in zip(tiles, raws, weighs):
            prob = e * inverse
            dscore = ((prob * scale) * (w_tile - delta)).astype(BF)
            prob = prob.astype(BF)
            if at.start < rows:
                inside, outside = sides_ref[0, at, cols], sides_ref[1, at, cols]
                p_ref[c, at, cols] = prob * inside
                ds_ref[c, far + at.start : far + at.stop, cols] = dscore * inside
                prob = prob * outside
                dscore = dscore * outside
            if at.start < 2 * rows:
                rest_ref[c, at, cols] = prob
            else:
                p_all[at.start - 2 * rows : at.stop - 2 * rows, cols] = prob
            ds_ref[c, at, cols] = dscore

    def head(c):
        for o in range(SPAN):
            k_all[o * rows : (o + 1) * rows, :] = kv_refs[o][c]
            v_all[o * rows : (o + 1) * rows, :] = kv_refs[o][kv_heads + c]
        for n in range(chunks):
            chunk(c, n)
        key_value_grads(ds_ref.at[c, 2 * rows : far], p_all, qr_ref.at[first + c], gr_ref.at[first + c], lanes_of(None, None, pair_ref)[2:], c)

    for c in range(kv_heads):
        head(c)


def rest_body(first, ds_ref, p_ref, qr_ref, gr_ref, far_ref, near_ref):
    part, count, _ = p_ref.shape
    for c in range(part):
        key_value_grads(ds_ref.at[c, :count], p_ref.at[c], qr_ref.at[first + c], gr_ref.at[first + c], (far_ref, near_ref), c)


def query_body(*refs):
    per = 6
    groups = [refs[per * i : per * (i + 1)] for i in range(CHUNKS)]
    qr_ref, gr_ref, dq_ref, own_ref, turned_ref = refs[per * CHUNKS :]
    kv_heads, lanes, depth = qr_ref.shape
    part = kv_heads // CHUNKS
    rows = dq_ref.shape[0]
    group = lanes // rows
    for c in range(kv_heads):
        *sent_refs, own_kv_ref, ds_ref, p_ref = groups[c // part]
        kv_refs = (*lanes_of(*sent_refs), own_kv_ref)
        at = c % part
        own_ref[c] = dot(ds_ref[at, SPAN * rows :, :], qr_ref[c], NN)
        own_ref[kv_heads + c] = dot(p_ref[at], gr_ref[c], NN)
        for o in range(SPAN + 1):
            turned_ref[:, o * rows : (o + 1) * rows] = kv_refs[o][at].astype(F32).T.astype(BF)
        dq = dot(turned_ref[...], ds_ref[at], NN).T
        dq_ref[:, c * group : (c + 1) * group, :] = dq.reshape(rows, group, depth).astype(BF)


def finish_body(own_ref, *refs):
    groups, (dk_ref, dv_ref, wide_ref) = [refs[3 * i : 3 * i + 3] for i in range(CHUNKS)], refs[3 * CHUNKS :]
    kv_heads, rows, _ = own_ref.shape
    kv_heads //= 2
    part = kv_heads // CHUNKS
    for half, out_ref in enumerate((dk_ref, dv_ref)):
        for c in range(kv_heads):
            total = own_ref[half * kv_heads + c]
            for ref in groups[c // part]:
                total = total + ref[half * part + c % part].astype(F32)
            wide_ref[half, pl.ds(c, rows, stride=kv_heads), :] = total
        out_ref[...] = wide_ref[half].astype(BF)


def per_device(queries, key_states, value_states, out_grad, bounds):
    rows, heads, depth = queries.shape
    kv_heads = key_states.shape[1]
    part = kv_heads // CHUNKS
    group = heads // kv_heads
    lanes = rows * group
    shape = jax.ShapeDtypeStruct
    my_index = lax.axis_index(AXES)
    odd = lax.rem(my_index, 2) == 1
    product = 2 * kv_heads * rows * lanes * depth
    block = shape((2 * part, rows, depth), BF)
    double = shape((4 * part, rows, depth), BF)
    zero = jnp.zeros(block.shape, BF)

    flat = shape((rows * kv_heads, depth), BF)
    owns = call(
        pack_body,
        (block,) * CHUNKS,
        (in_hbm(key_states.reshape(flat.shape)), in_hbm(value_states.reshape(flat.shape))),
        specs=[HBM] * 2,
        scratch=(pltpu.VMEM((2, *flat.shape), BF), pltpu.VMEM((2, *flat.shape), F32), pltpu.SemaphoreType.DMA((2,))),
    )
    sent = []
    for own in owns:
        sent.append(rotated_pair((own, own), 1))
    ready = call(
        prepare_body,
        (
            shape((kv_heads, lanes, depth), BF),
            shape((kv_heads, lanes, depth), BF),
            shape((SPAN * rows, lanes), F32),
            shape((rows, lanes), F32),
            shape((2, rows, lanes), BF),
            shape((kv_heads, rows, lanes), F32),
            shape((kv_heads, rows, lanes), F32),
        ),
        (my_index.reshape(1), in_hbm(queries), in_hbm(out_grad), in_hbm(bounds), *owns),
        specs=[SMEM, HBM, HBM, HBM] + [VMEM] * CHUNKS,
        scratch=(pltpu.VMEM(queries.shape, BF), pltpu.VMEM(queries.shape, BF), pltpu.VMEM(bounds.shape, jnp.int32), pltpu.VMEM((2, rows, lanes), F32), pltpu.SemaphoreType.DMA((3,))),
        flops=2 * product,
    )
    qr, gr = ready[:2]
    blocks, scores, backs, rests = [], [], [], []
    back = None
    for i in range(CHUNKS):
        (far, near), ready = lax.optimization_barrier((sent[i], ready))
        pair = swapped(jnp.concatenate([near, jnp.where(odd, far, owns[i])]))
        if back is not None:
            pair, back = lax.optimization_barrier((pair, back))
            backs.append(rotated_pair(back, -1))
        g_pair, dscore, prob, rest = call(
            functools.partial(main_body, i * part),
            (
                double,
                shape((part, (SPAN + 1) * rows, lanes), BF),
                shape((part, rows, lanes), BF),
                shape((part, 2 * rows, lanes), BF),
            ),
            (far, near, pair, *ready),
            scratch=(
                pltpu.VMEM((SPAN * rows, depth), BF),
                pltpu.VMEM((SPAN * rows, depth), BF),
                pltpu.VMEM((2 * rows, lanes), BF),
            ),
            flops=16 * product // CHUNKS,
            mib=20,
        )
        blocks.append((far, near, pair, owns[i]))
        scores.append((dscore, prob))
        if i + 1 < CHUNKS:
            sent[i + 1], g_pair = lax.optimization_barrier((sent[i + 1], g_pair))
        turned = swapped(g_pair)
        g_far, g_near = call(
            functools.partial(rest_body, i * part), (block, block), (dscore, rest, qr, gr), flops=2 * product // CHUNKS
        )
        back_x, back_y = jnp.split(turned, 2)
        back = (
            (g_far.astype(F32) + jnp.where(odd, back_y, zero).astype(F32)).astype(BF),
            (g_near.astype(F32) + back_x.astype(F32)).astype(BF),
        )
        rests.append(jnp.where(odd, zero, back_y))
    back, scores[-1] = lax.optimization_barrier((back, scores[-1]))
    backs.append(rotated_pair(back, -1))
    inputs = []
    for block_refs, score in zip(blocks, scores):
        inputs += [*block_refs, *score]
    dq, own_sum = call(
        query_body,
        (shape((rows, heads, depth), BF), shape((2 * kv_heads, rows, depth), F32)),
        (*inputs, qr, gr),
        scratch=(pltpu.VMEM((depth, (SPAN + 1) * rows), BF),),
        flops=7 * product,
    )
    inputs = []
    for rest, got in zip(rests, backs):
        inputs += [rest, *got]
    dk, dv = call(finish_body, (flat, flat), (own_sum, *inputs), scratch=(pltpu.VMEM((2, *flat.shape), F32),))
    return dq, dk.reshape(key_states.shape), dv.reshape(value_states.shape)


def solution(mesh):
    rows = P(AXES, None, None)

    return jax.shard_map(
        per_device,
        mesh=mesh,
        in_specs=(rows, rows, rows, rows, P(None, AXES)),
        out_specs=(rows, rows, rows),
        check_vma=False,
    )
```

profile of v0, /device:TPU:2, one launch (start us, length us, event | category | flops | bytes accessed | tf_op | source)
XLA Modules:
  0.0 46.3 jit_solution(10413496238812730599)
XLA Ops:
  0.6 1.0 %shard_map.76 = (bf16[4,128,128]{2,1,0:T(8,128)(2,1)S(1)}, bf16[4,128,128]{2,1,0:T(8,128)(2,1)S(1)}) custom-call(bf16[512,128]{1,0:T(8,128)(2,1)} %bitcast.5, bf16[512,128]{1,0:T(8,128)(2,1)} %bitcast.6), custom_call_target="tpu_custom_call" | custom-call | bytes 1048576 | tf_op jit(solution)/shard_map/pallas_call | solution.py:52
  1.7 1.5 %collective-permute-start.1 = (bf16[4,128,128]{2,1,0:T(8,128)(2,1)S(1)}, bf16[4,128,128]{2,1,0:T(8,128)(2,1)S(1)}, u32[]{:S(2)}, u32[]{:S(2)}) collective-permute-start(bf16[4,128,128]{2,1,0:T(8,128)(2,1)S(1)} %get-tuple-element.56.refs_0_.refs_3_), channel_id=1, source_target_pairs={{0,2},{1,3},{2,4},{3,5},{4,6},{5,7},{6,8},{7,9},{8,10},{9,11},{10,... | collective-permute-start | bytes 393224 | tf_op jit(solution)/shard_map/ppermute | solution.py:29
  3.2 1.5 %collective-permute-start = (bf16[4,128,128]{2,1,0:T(8,128)(2,1)S(1)}, bf16[4,128,128]{2,1,0:T(8,128)(2,1)S(1)}, u32[]{:S(2)}, u32[]{:S(2)}) collective-permute-start(bf16[4,128,128]{2,1,0:T(8,128)(2,1)S(1)} %get-tuple-element.56.refs_0_.refs_3_), channel_id=1, source_target_pairs={{0,4},{1,5},{2,6},{3,7},{4,8},{5,9},{6,10},{7,11},{8,12},{9,13},{1... | collective-permute-start | bytes 393224 | tf_op jit(solution)/shard_map/ppermute | solution.py:29
  4.7 2.7 %shard_map.77 = (bf16[4,1024,128]{2,1,0:T(8,128)(2,1)S(1)}, bf16[4,1024,128]{2,1,0:T(8,128)(2,1)S(1)}, f32[512,1024]{1,0:T(8,128)S(1)}, f32[128,1024]{1,0:T(8,12...) custom-call(s32[1]{0:T(128)} %bitcast.2.me_ref, ...), custom_call_target="tpu_custom_call" | custom-call | flops 268435456 | bytes 1048576 | tf_op jit(solution)/shard_map/pallas_call | solution.py:52
  7.4 0.0 collective-permute-done.1.refs_1_
  7.4 5.1 %collective-permute-done.refs_0_ = bf16[4,128,128]{2,1,0:T(8,128)(2,1)S(1)} collective-permute-done((bf16[4,128,128]{2,1,0:T(8,128)(2,1)S(1)}, bf16[4,128,128]{2,1,0:T(8,128)(2,1)S(1)}, u32[]{:S(2)}, u32[]{:S(2)}) %collective-permute-start) | collective-permute-done | bytes 131104 | tf_op jit(solution)/shard_map/ppermute | solution.py:29
  12.6 0.1 collective-permute-start.2
  12.7 0.1 collective-permute-start.4
  12.8 2.0 %collective-permute-start.3 = (bf16[4,128,128]{2,1,0:T(8,128)(2,1)S(1)}, bf16[4,128,128]{2,1,0:T(8,128)(2,1)S(1)}, u32[]{:S(2)}, u32[]{:S(2)}) collective-permute-start(bf16[4,128,128]{2,1,0:T(8,128)(2,1)S(1)} %get-tuple-element.57.refs_1_.refs_9_), channel_id=1, source_target_pairs={{0,4},{1,5},{2,6},{3,7},{4,8},{5,9},{6,10},{7,11},{8,12},{9,13},{1... | collective-permute-start | bytes 393224 | tf_op jit(solution)/shard_map/ppermute | solution.py:29
  14.8 3.9 %shard_map.78 = (bf16[8,128,128]{2,1,0:T(8,128)(2,1)S(1)}, bf16[2,640,1024]{2,1,0:T(8,128)(2,1)S(1)}, bf16[2,128,1024]{2,1,0:T(8,128)(2,1)S(1)}, bf16[2,256,1024]{2,1,0:T(8,128)(2,1)S(1)}) custom-call(bf16[4,128,128]{2,1,0:T(8,128)(2,1)S(1)} %collective-permute-done.refs_0_, bf16[4,128,128]{2,1,0:T(8,128)(2,1)S(1)} %collective-permute-done.1.refs_1_, ...), custom_call_target="tpu_custom_call" | custom-call | flops 1073741824 | bytes 1048576 | tf_op jit(solution)/shard_map/pallas_call | solution.py:52
  18.7 0.0 collective-permute-done.4.refs_1_.refs_7_
  18.7 6.6 %collective-permute-done.3.refs_0_.refs_6_ = bf16[4,128,128]{2,1,0:T(8,128)(2,1)S(1)} collective-permute-done((bf16[4,128,128]{2,1,0:T(8,128)(2,1)S(1)}, bf16[4,128,128]{2,1,0:T(8,128)(2,1)S(1)}, u32[]{:S(2)}, u32[]{:S(2)}) %collective-permute-start.3) | collective-permute-done | bytes 131104 | tf_op jit(solution)/shard_map/ppermute | solution.py:29
  25.3 0.0 collective-permute-start.6
  25.3 0.6 %collective-permute-start.5 = (bf16[8,128,128]{2,1,0:T(8,128)(2,1)S(1)}, bf16[8,128,128]{2,1,0:T(8,128)(2,1)S(1)}, u32[]{:S(2)}, u32[]{:S(2)}) collective-permute-start(bf16[8,128,128]{2,1,0:T(8,128)(2,1)S(1)} %pad_maximum_fusion.1), channel_id=1, source_target_pairs={{0,1},{1,0},{2,3},{3,2},{4,5},{5,4},{6,7},{7,6},{8,9},{9,8},{10,11... | collective-permute-start | bytes 786440 | tf_op jit(solution)/shard_map/ppermute | solution.py:40
  25.9 0.7 %shard_map.79 = (bf16[4,128,128]{2,1,0:T(8,128)(2,1)S(1)}, bf16[4,128,128]{2,1,0:T(8,128)(2,1)S(1)}) custom-call(bf16[2,640,1024]{2,1,0:T(8,128)(2,1)S(1)} %get-tuple-element.74.ds_ref.refs_4_, bf16[2,256,1024]{2,1,0:T(8,128)(2,1)S(1)} %get-tuple-element.81.p_ref, bf16[4,1024,128]{2,1,0:T(8,128)(2,1)S(1)} %get-tuple-element.86.refs_3_.qr_ref.refs_12_, ...), custom_call_target="tpu_custom_call" | custom-call | flops 134217728 | bytes 1048576 | tf_op jit(solution)/shard_map/pallas_call | solution.py:52
  26.6 0.2 collective-permute-done.6
  26.8 0.1 add_convert_fusion.2
  26.9 0.3 collective-permute-done.5.refs_2_.refs_8_
  27.2 3.9 %shard_map.80 = (bf16[8,128,128]{2,1,0:T(8,128)(2,1)S(1)}, bf16[2,640,1024]{2,1,0:T(8,128)(2,1)S(1)}, bf16[2,128,1024]{2,1,0:T(8,128)(2,1)S(1)}, bf16[2,256,1024]{2,1,0:T(8,128)(2,1)S(1)}) custom-call(bf16[4,128,128]{2,1,0:T(8,128)(2,1)S(1)} %collective-permute-done.3.refs_0_.refs_6_, bf16[4,128,128]{2,1,0:T(8,128)(2,1)S(1)} %collective-permute-done.4.refs_1_.refs_7_, ...), custom_call_target="tpu_custom_call" | custom-call | flops 1073741824 | bytes 1048576 | tf_op jit(solution)/shard_map/pallas_call | solution.py:52
  31.1 0.3 collective-permute-start.7
  31.4 0.0 collective-permute-start.8
  31.5 0.6 %collective-permute-start.9 = (bf16[4,128,128]{2,1,0:T(8,128)(2,1)S(1)}, bf16[4,128,128]{2,1,0:T(8,128)(2,1)S(1)}, u32[]{:S(2)}, u32[]{:S(2)}) collective-permute-start(bf16[4,128,128]{2,1,0:T(8,128)(2,1)S(1)} %get-tuple-element.104), channel_id=1, source_target_pairs={{0,30},{1,31},{2,0},{3,1},{4,2},{5,3},{6,4},{7,5},{8,6},{9,7},{10,... | collective-permute-start | bytes 393224 | tf_op jit(solution)/shard_map/ppermute | solution.py:29
  32.0 0.7 %shard_map.81 = (bf16[4,128,128]{2,1,0:T(8,128)(2,1)S(1)}, bf16[4,128,128]{2,1,0:T(8,128)(2,1)S(1)}) custom-call(bf16[2,640,1024]{2,1,0:T(8,128)(2,1)S(1)} %get-tuple-element.99.ds_ref.refs_10_, bf16[2,256,1024]{2,1,0:T(8,128)(2,1)S(1)} %get-tuple-element.94.p_ref, bf16[4,1024,128]{2,1,0:T(8,128)(2,1)S(1)} %get-tuple-element.86.refs_3_.qr_ref.refs_12_, ...), custom_call_target="tpu_custom_call" | custom-call | flops 134217728 | bytes 1048576 | tf_op jit(solution)/shard_map/pallas_call | solution.py:52
  32.8 0.0 collective-permute-done.7
  32.8 0.1 add_convert_fusion
  32.9 1.4 %collective-permute-start.10 = (bf16[4,128,128]{2,1,0:T(8,128)(2,1)S(1)}, bf16[4,128,128]{2,1,0:T(8,128)(2,1)S(1)}, u32[]{:S(2)}, u32[]{:S(2)}) collective-permute-start(bf16[4,128,128]{2,1,0:T(8,128)(2,1)S(1)} %get-tuple-element.105), channel_id=1, source_target_pairs={{0,28},{1,29},{2,30},{3,31},{4,0},{5,1},{6,2},{7,3},{8,4},{9,5},{1... | collective-permute-start | bytes 393224 | tf_op jit(solution)/shard_map/ppermute | solution.py:29
  34.2 0.9 %collective-permute-start.11 = (bf16[4,128,128]{2,1,0:T(8,128)(2,1)S(1)}, bf16[4,128,128]{2,1,0:T(8,128)(2,1)S(1)}, u32[]{:S(2)}, u32[]{:S(2)}) collective-permute-start(bf16[4,128,128]{2,1,0:T(8,128)(2,1)S(1)} %get-tuple-element.106), channel_id=1, source_target_pairs={{0,30},{1,31},{2,0},{3,1},{4,2},{5,3},{6,4},{7,5},{8,6},{9,7},{10,... | collective-permute-start | bytes 393224 | tf_op jit(solution)/shard_map/ppermute | solution.py:29
  35.2 2.6 %shard_map.82 = (bf16[128,32,128]{2,1,0:T(8,128)(2,1)}, f32[8,128,128]{2,1,0:T(8,128)S(1)}) custom-call(bf16[4,128,128]{2,1,0:T(8,128)(2,1)S(1)} %collective-permute-done.refs_0_, bf16[4,128,128]{2,1,0:T(8,128)(2,1)S(1)} %collective-permute-done.1.refs_1_, bf16[8,128,128]{2,1,0:T(8,128)(2,1)S(1)} %collective-permute-done.2.refs_2_, ...), custom_call_target="tpu_custom_call" | custom-call | flops 939524096 | bytes 1048576 | tf_op jit(solution)/shard_map/pallas_call | solution.py:52
  37.8 5.7 %collective-permute-done.8.refs_1_ = bf16[4,128,128]{2,1,0:T(8,128)(2,1)S(1)} collective-permute-done((bf16[4,128,128]{2,1,0:T(8,128)(2,1)S(1)}, bf16[4,128,128]{2,1,0:T(8,128)(2,1)S(1)}, u32[]{:S(2)}, u32[]{:S(2)}) %collective-permute-start.8) | collective-permute-done | bytes 131104 | tf_op jit(solution)/shard_map/ppermute | solution.py:29
  43.4 0.0 collective-permute-done.9.refs_2_
  43.4 2.1 %collective-permute-done.10.refs_4_ = bf16[4,128,128]{2,1,0:T(8,128)(2,1)S(1)} collective-permute-done((bf16[4,128,128]{2,1,0:T(8,128)(2,1)S(1)}, bf16[4,128,128]{2,1,0:T(8,128)(2,1)S(1)}, u32[]{:S(2)}, u32[]{:S(2)}) %collective-permute-start.10) | collective-permute-done | bytes 131104 | tf_op jit(solution)/shard_map/ppermute | solution.py:29
  45.5 0.8 %shard_map.83 = (bf16[512,128]{1,0:T(8,128)(2,1)}, bf16[512,128]{1,0:T(8,128)(2,1)}) custom-call(f32[8,128,128]{2,1,0:T(8,128)S(1)} %get-tuple-element.102.own_ref, bf16[4,128,128]{2,1,0:T(8,128)(2,1)S(1)} %broadcast_select_fusion.1.refs_0_, bf16[4,128,128]{2,1,0:T(8,128)(2,1)S(1)} %collective-permute-done.8.refs_1_, ...), custom_call_target="tpu_custom_call" | custom-call | bytes 1048576 | tf_op jit(solution)/shard_map/pallas_call | solution.py:52
  (8 shorter events, 0.1 us)
Async XLA Ops:
  1.7 5.8 %collective-permute-start.1 = (bf16[4,128,128]{2,1,0:T(8,128)(2,1)S(1)}, bf16[4,128,128]{2,1,0:T(8,128)(2,1)S(1)}, u32[]{:S(2)}, u32[]{:S(2)}) collective-permute-start(bf16[4,128,128]{2,1,0:T(8,128)(2,1)S(1)} %get-tuple-element.56.refs_0_.refs_3_), channel_id=1, source_target_pairs={{0,2},{1,3},{2,4},{3,5},{4,6},{5,7},{6,8},{7,9},{8,10},{9,11},{10,... | collective-permute-start | bytes 393224 | tf_op jit(solution)/shard_map/ppermute | solution.py:29
  3.2 9.4 %collective-permute-start = (bf16[4,128,128]{2,1,0:T(8,128)(2,1)S(1)}, bf16[4,128,128]{2,1,0:T(8,128)(2,1)S(1)}, u32[]{:S(2)}, u32[]{:S(2)}) collective-permute-start(bf16[4,128,128]{2,1,0:T(8,128)(2,1)S(1)} %get-tuple-element.56.refs_0_.refs_3_), channel_id=1, source_target_pairs={{0,4},{1,5},{2,6},{3,7},{4,8},{5,9},{6,10},{7,11},{8,12},{9,13},{1... | collective-permute-start | bytes 393224 | tf_op jit(solution)/shard_map/ppermute | solution.py:29
  12.6 2.1 %collective-permute-start.2 = (bf16[8,128,128]{2,1,0:T(8,128)(2,1)S(1)}, bf16[8,128,128]{2,1,0:T(8,128)(2,1)S(1)}, u32[]{:S(2)}, u32[]{:S(2)}) collective-permute-start(bf16[8,128,128]{2,1,0:T(8,128)(2,1)S(1)} %pad_maximum_fusion), channel_id=1, source_target_pairs={{0,1},{1,0},{2,3},{3,2},{4,5},{5,4},{6,7},{7,6},{8,9},{9,8},{10,11... | collective-permute-start | bytes 786440 | tf_op jit(solution)/shard_map/ppermute | solution.py:40
  12.7 6.0 %collective-permute-start.4 = (bf16[4,128,128]{2,1,0:T(8,128)(2,1)S(1)}, bf16[4,128,128]{2,1,0:T(8,128)(2,1)S(1)}, u32[]{:S(2)}, u32[]{:S(2)}) collective-permute-start(bf16[4,128,128]{2,1,0:T(8,128)(2,1)S(1)} %get-tuple-element.57.refs_1_.refs_9_), channel_id=1, source_target_pairs={{0,2},{1,3},{2,4},{3,5},{4,6},{5,7},{6,8},{7,9},{8,10},{9,11},{10,... | collective-permute-start | bytes 393224 | tf_op jit(solution)/shard_map/ppermute | solution.py:29
  12.8 12.5 %collective-permute-start.3 = (bf16[4,128,128]{2,1,0:T(8,128)(2,1)S(1)}, bf16[4,128,128]{2,1,0:T(8,128)(2,1)S(1)}, u32[]{:S(2)}, u32[]{:S(2)}) collective-permute-start(bf16[4,128,128]{2,1,0:T(8,128)(2,1)S(1)} %get-tuple-element.57.refs_1_.refs_9_), channel_id=1, source_target_pairs={{0,4},{1,5},{2,6},{3,7},{4,8},{5,9},{6,10},{7,11},{8,12},{9,13},{1... | collective-permute-start | bytes 393224 | tf_op jit(solution)/shard_map/ppermute | solution.py:29
  25.3 1.5 %collective-permute-start.6 = (bf16[8,128,128]{2,1,0:T(8,128)(2,1)S(1)}, bf16[8,128,128]{2,1,0:T(8,128)(2,1)S(1)}, u32[]{:S(2)}, u32[]{:S(2)}) collective-permute-start(bf16[8,128,128]{2,1,0:T(8,128)(2,1)S(1)} %get-tuple-element.83), channel_id=1, source_target_pairs={{0,1},{1,0},{2,3},{3,2},{4,5},{5,4},{6,7},{7,6},{8,9},{9,8},{10,11... | collective-permute-start | bytes 786440 | tf_op jit(solution)/shard_map/ppermute | solution.py:40
  25.3 1.9 %collective-permute-start.5 = (bf16[8,128,128]{2,1,0:T(8,128)(2,1)S(1)}, bf16[8,128,128]{2,1,0:T(8,128)(2,1)S(1)}, u32[]{:S(2)}, u32[]{:S(2)}) collective-permute-start(bf16[8,128,128]{2,1,0:T(8,128)(2,1)S(1)} %pad_maximum_fusion.1), channel_id=1, source_target_pairs={{0,1},{1,0},{2,3},{3,2},{4,5},{5,4},{6,7},{7,6},{8,9},{9,8},{10,11... | collective-permute-start | bytes 786440 | tf_op jit(solution)/shard_map/ppermute | solution.py:40
  31.1 1.6 %collective-permute-start.7 = (bf16[8,128,128]{2,1,0:T(8,128)(2,1)S(1)}, bf16[8,128,128]{2,1,0:T(8,128)(2,1)S(1)}, u32[]{:S(2)}, u32[]{:S(2)}) collective-permute-start(bf16[8,128,128]{2,1,0:T(8,128)(2,1)S(1)} %get-tuple-element.96), channel_id=1, source_target_pairs={{0,1},{1,0},{2,3},{3,2},{4,5},{5,4},{6,7},{7,6},{8,9},{9,8},{10,11... | collective-permute-start | bytes 786440 | tf_op jit(solution)/shard_map/ppermute | solution.py:40
  31.4 12.0 %collective-permute-start.8 = (bf16[4,128,128]{2,1,0:T(8,128)(2,1)S(1)}, bf16[4,128,128]{2,1,0:T(8,128)(2,1)S(1)}, u32[]{:S(2)}, u32[]{:S(2)}) collective-permute-start(bf16[4,128,128]{2,1,0:T(8,128)(2,1)S(1)} %get-tuple-element.103), channel_id=1, source_target_pairs={{0,28},{1,29},{2,30},{3,31},{4,0},{5,1},{6,2},{7,3},{8,4},{9,5},{1... | collective-permute-start | bytes 393224 | tf_op jit(solution)/shard_map/ppermute | solution.py:29
  31.5 12.0 %collective-permute-start.9 = (bf16[4,128,128]{2,1,0:T(8,128)(2,1)S(1)}, bf16[4,128,128]{2,1,0:T(8,128)(2,1)S(1)}, u32[]{:S(2)}, u32[]{:S(2)}) collective-permute-start(bf16[4,128,128]{2,1,0:T(8,128)(2,1)S(1)} %get-tuple-element.104), channel_id=1, source_target_pairs={{0,30},{1,31},{2,0},{3,1},{4,2},{5,3},{6,4},{7,5},{8,6},{9,7},{10,... | collective-permute-start | bytes 393224 | tf_op jit(solution)/shard_map/ppermute | solution.py:29
  32.9 12.7 %collective-permute-start.10 = (bf16[4,128,128]{2,1,0:T(8,128)(2,1)S(1)}, bf16[4,128,128]{2,1,0:T(8,128)(2,1)S(1)}, u32[]{:S(2)}, u32[]{:S(2)}) collective-permute-start(bf16[4,128,128]{2,1,0:T(8,128)(2,1)S(1)} %get-tuple-element.105), channel_id=1, source_target_pairs={{0,28},{1,29},{2,30},{3,31},{4,0},{5,1},{6,2},{7,3},{8,4},{9,5},{1... | collective-permute-start | bytes 393224 | tf_op jit(solution)/shard_map/ppermute | solution.py:29
  34.2 11.3 %collective-permute-start.11 = (bf16[4,128,128]{2,1,0:T(8,128)(2,1)S(1)}, bf16[4,128,128]{2,1,0:T(8,128)(2,1)S(1)}, u32[]{:S(2)}, u32[]{:S(2)}) collective-permute-start(bf16[4,128,128]{2,1,0:T(8,128)(2,1)S(1)} %get-tuple-element.106), channel_id=1, source_target_pairs={{0,30},{1,31},{2,0},{3,1},{4,2},{5,3},{6,4},{7,5},{8,6},{9,7},{10,... | collective-permute-start | bytes 393224 | tf_op jit(solution)/shard_map/ppermute | solution.py:29
where the time goes:
time: 46.5 us; the launch traced here: 46.3 us
  waiting for transfers between devices  20 us (43%)
  Pallas kernels  16.4 us (35%)
  starting transfers between devices  8.97 us (19%)
  between operations  0.76 us (2%)
    ppermute x8, waiting for transfers between devices, rotated(): lax.ppermute(shard, AXES, [(i, (i + by) % peers) for i in range(peers)])  19.5 us
    pallas_call x8, Pallas kernels, call(): pl.pallas_call(body, out_shape=outs, in_specs=specs or [VMEM] * len(args)...  16.4 us
    ppermute x8, starting transfers between devices, rotated(): lax.ppermute(shard, AXES, [(i, (i + by) % peers) for i in range(peers)])  8 us
    ppermute x4, starting transfers between devices, swapped(): return lax.ppermute(shard, AXES, [(i, i ^ 1) for i in range(peers)])  0.97 us
  transfers between devices with their start and end apart: 12, of which 6 were waited for; matrix products, arithmetic and copies ran while one was open for 1% of the time, Pallas kernels for 23%

commit v1 on v0

--- a/solution.py
+++ b/solution.py
@@ -80,11 +80,10 @@
             kv_refs[c // part][half * part + c % part] = wide_ref[half, pl.ds(c, rows, stride=heads), :].astype(BF)
 
 
-def prepare_body(me_ref, q_hbm, g_hbm, bounds_hbm, *refs):
+def prepare_body(me_ref, q_hbm, g_hbm, bounds_ref, *refs):
     kv_refs, outs = refs[:CHUNKS], refs[CHUNKS:]
-    qr_ref, gr_ref, bias_ref, outside_ref, sides_ref, s_ref, w_ref, q_ref, g_ref, bounds_ref, inside_ref, sems = outs
-    first, *copies = fetch((bounds_hbm, q_hbm, g_hbm), (bounds_ref, q_ref, g_ref), sems)
-    first.wait()
+    qr_ref, gr_ref, bias_ref, outside_ref, sides_ref, s_ref, w_ref, q_ref, g_ref, inside_ref, sems = outs
+    copies = fetch((q_hbm, g_hbm), (q_ref, g_ref), sems)
     rows, heads, depth = q_ref.shape
     kv_heads = qr_ref.shape[0]
     part = kv_heads // CHUNKS
@@ -286,16 +285,16 @@
             shape((kv_heads, rows, lanes), F32),
             shape((kv_heads, rows, lanes), F32),
         ),
-        (my_index.reshape(1), in_hbm(queries), in_hbm(out_grad), in_hbm(bounds), *owns),
-        specs=[SMEM, HBM, HBM, HBM] + [VMEM] * CHUNKS,
-        scratch=(pltpu.VMEM(queries.shape, BF), pltpu.VMEM(queries.shape, BF), pltpu.VMEM(bounds.shape, jnp.int32), pltpu.VMEM((2, rows, lanes), F32), pltpu.SemaphoreType.DMA((3,))),
+        (my_index.reshape(1), in_hbm(queries), in_hbm(out_grad), bounds, *owns),
+        specs=[SMEM, HBM, HBM] + [VMEM] * (1 + CHUNKS),
+        scratch=(pltpu.VMEM(queries.shape, BF), pltpu.VMEM(queries.shape, BF), pltpu.VMEM((2, rows, lanes), F32), pltpu.SemaphoreType.DMA((2,))),
         flops=2 * product,
     )
     qr, gr = ready[:2]
     blocks, scores, backs, rests = [], [], [], []
     back = None
     for i in range(CHUNKS):
-        (far, near), ready = lax.optimization_barrier((sent[i], ready))
+        far, near = sent[i]
         pair = swapped(jnp.concatenate([near, jnp.where(odd, far, owns[i])]))
         if back is not None:
             pair, back = lax.optimization_barrier((pair, back))

time: 46.5 us -> 46.5 us (level)
  waiting for transfers between devices: 20 us -> 16.3 us
  starting transfers between devices: 8.97 us -> 12 us
  local copies, waits for them, and re-layouts: 0 us -> 0.68 us
    ppermute x8, waiting for transfers between devices: 19.5 us -> 15.8 us  [rotated(): lax.ppermute(shard, AXES, [(i, (i + by) % peers) for i in range(peers)])]
    ppermute x8, starting transfers between devices: 8 us -> 11 us  [rotated(): lax.ppermute(shard, AXES, [(i, (i + by) % peers) for i in range(peers)])]
    unnamed x0 -> x2, local copies, waits for them, and re-layouts: none -> 0.68 us
where the time goes in v1:
time: 46.5 us; the launch traced here: 46.3 us
  Pallas kernels  16.3 us (35%)
  waiting for transfers between devices  16.3 us (35%)
  starting transfers between devices  12 us (26%)
  between operations  0.76 us (2%)
  local copies, waits for them, and re-layouts  0.68 us (1%)
    pallas_call x8, Pallas kernels, call(): pl.pallas_call(body, out_shape=outs, in_specs=specs or [VMEM] * len(args)...  16.3 us
    ppermute x8, waiting for transfers between devices, rotated(): lax.ppermute(shard, AXES, [(i, (i + by) % peers) for i in range(peers)])  15.8 us
    ppermute x8, starting transfers between devices, rotated(): lax.ppermute(shard, AXES, [(i, (i + by) % peers) for i in range(peers)])  11 us
    ppermute x4, starting transfers between devices, swapped(): return lax.ppermute(shard, AXES, [(i, i ^ 1) for i in range(peers)])  0.97 us
  transfers between devices with their start and end apart: 12, of which 6 were waited for; matrix products, arithmetic and copies ran while one was open for 1% of the time, Pallas kernels for 23%

profile of v1, /device:TPU:2, one launch (start us, length us, event | category | flops | bytes accessed | tf_op | source)
XLA Modules:
  0.0 46.3 jit_solution(12949039595298913209)
XLA Ops:
  0.6 1.0 %shard_map.76 = (bf16[4,128,128]{2,1,0:T(8,128)(2,1)S(1)}, bf16[4,128,128]{2,1,0:T(8,128)(2,1)S(1)}) custom-call(bf16[512,128]{1,0:T(8,128)(2,1)} %bitcast.5, bf16[512,128]{1,0:T(8,128)(2,1)} %bitcast.6), custom_call_target="tpu_custom_call" | custom-call | bytes 1048576 | tf_op jit(solution)/shard_map/pallas_call | solution.py:52
  1.7 1.6 %collective-permute-start = (bf16[4,128,128]{2,1,0:T(8,128)(2,1)S(1)}, bf16[4,128,128]{2,1,0:T(8,128)(2,1)S(1)}, u32[]{:S(2)}, u32[]{:S(2)}) collective-permute-start(bf16[4,128,128]{2,1,0:T(8,128)(2,1)S(1)} %get-tuple-element.38.refs_0_.refs_3_), channel_id=1, source_target_pairs={{0,4},{1,5},{2,6},{3,7},{4,8},{5,9},{6,10},{7,11},{8,12},{9,13},{1... | collective-permute-start | bytes 393224 | tf_op jit(solution)/shard_map/ppermute | solution.py:29
  3.2 1.5 %collective-permute-start.1 = (bf16[4,128,128]{2,1,0:T(8,128)(2,1)S(1)}, bf16[4,128,128]{2,1,0:T(8,128)(2,1)S(1)}, u32[]{:S(2)}, u32[]{:S(2)}) collective-permute-start(bf16[4,128,128]{2,1,0:T(8,128)(2,1)S(1)} %get-tuple-element.38.refs_0_.refs_3_), channel_id=1, source_target_pairs={{0,2},{1,3},{2,4},{3,5},{4,6},{5,7},{6,8},{7,9},{8,10},{9,11},{10,... | collective-permute-start | bytes 393224 | tf_op jit(solution)/shard_map/ppermute | solution.py:29
  4.7 6.1 %collective-permute-done.refs_0_ = bf16[4,128,128]{2,1,0:T(8,128)(2,1)S(1)} collective-permute-done((bf16[4,128,128]{2,1,0:T(8,128)(2,1)S(1)}, bf16[4,128,128]{2,1,0:T(8,128)(2,1)S(1)}, u32[]{:S(2)}, u32[]{:S(2)}) %collective-permute-start) | collective-permute-done | bytes 131104 | tf_op jit(solution)/shard_map/ppermute | solution.py:29
  10.8 0.0 collective-permute-done.1.refs_1_
  10.8 0.1 collective-permute-start.2
  10.9 0.5 %collective-permute-start.4 = (bf16[4,128,128]{2,1,0:T(8,128)(2,1)S(1)}, bf16[4,128,128]{2,1,0:T(8,128)(2,1)S(1)}, u32[]{:S(2)}, u32[]{:S(2)}) collective-permute-start(bf16[4,128,128]{2,1,0:T(8,128)(2,1)S(1)} %get-tuple-element.39.refs_1_.refs_9_), channel_id=1, source_target_pairs={{0,2},{1,3},{2,4},{3,5},{4,6},{5,7},{6,8},{7,9},{8,10},{9,11},{10,... | collective-permute-start | bytes 393224 | tf_op jit(solution)/shard_map/ppermute | solution.py:29
  11.4 3.3 %collective-permute-start.3 = (bf16[4,128,128]{2,1,0:T(8,128)(2,1)S(1)}, bf16[4,128,128]{2,1,0:T(8,128)(2,1)S(1)}, u32[]{:S(2)}, u32[]{:S(2)}) collective-permute-start(bf16[4,128,128]{2,1,0:T(8,128)(2,1)S(1)} %get-tuple-element.39.refs_1_.refs_9_), channel_id=1, source_target_pairs={{0,4},{1,5},{2,6},{3,7},{4,8},{5,9},{6,10},{7,11},{8,12},{9,13},{1... | collective-permute-start | bytes 393224 | tf_op jit(solution)/shard_map/ppermute | solution.py:29
  14.8 0.7 %copy-done = s32[3,128]{1,0:T(4,128)S(1)} copy-done((s32[3,128]{1,0:T(4,128)S(1)}, s32[3,128]{1,0:T(4,128)}, u32[]{:S(2)}) %copy-start) | copy-done | bytes 1560
  15.4 2.7 %shard_map.77 = (bf16[4,1024,128]{2,1,0:T(8,128)(2,1)S(1)}, bf16[4,1024,128]{2,1,0:T(8,128)(2,1)S(1)}, f32[512,1024]{1,0:T(8,128)S(1)}, f32[128,1024]{1,0:T(8,12...) custom-call(s32[1]{0:T(128)} %bitcast.2.me_ref, ...), custom_call_target="tpu_custom_call" | custom-call | flops 268435456 | bytes 1048576 | tf_op jit(solution)/shard_map/pallas_call | solution.py:52
  18.1 3.9 %shard_map.78 = (bf16[8,128,128]{2,1,0:T(8,128)(2,1)S(1)}, bf16[2,640,1024]{2,1,0:T(8,128)(2,1)S(1)}, bf16[2,128,1024]{2,1,0:T(8,128)(2,1)S(1)}, bf16[2,256,1024]{2,1,0:T(8,128)(2,1)S(1)}) custom-call(bf16[4,128,128]{2,1,0:T(8,128)(2,1)S(1)} %collective-permute-done.refs_0_, bf16[4,128,128]{2,1,0:T(8,128)(2,1)S(1)} %collective-permute-done.1.refs_1_, ...), custom_call_target="tpu_custom_call" | custom-call | flops 1073741824 | bytes 1048576 | tf_op jit(solution)/shard_map/pallas_call | solution.py:52
  22.1 0.0 collective-permute-done.4.refs_1_.refs_7_
  22.1 3.2 %collective-permute-done.3.refs_0_.refs_6_ = bf16[4,128,128]{2,1,0:T(8,128)(2,1)S(1)} collective-permute-done((bf16[4,128,128]{2,1,0:T(8,128)(2,1)S(1)}, bf16[4,128,128]{2,1,0:T(8,128)(2,1)S(1)}, u32[]{:S(2)}, u32[]{:S(2)}) %collective-permute-start.3) | collective-permute-done | bytes 131104 | tf_op jit(solution)/shard_map/ppermute | solution.py:29
  25.3 0.0 collective-permute-start.6
  25.3 0.6 %collective-permute-start.5 = (bf16[8,128,128]{2,1,0:T(8,128)(2,1)S(1)}, bf16[8,128,128]{2,1,0:T(8,128)(2,1)S(1)}, u32[]{:S(2)}, u32[]{:S(2)}) collective-permute-start(bf16[8,128,128]{2,1,0:T(8,128)(2,1)S(1)} %pad_maximum_fusion.1), channel_id=1, source_target_pairs={{0,1},{1,0},{2,3},{3,2},{4,5},{5,4},{6,7},{7,6},{8,9},{9,8},{10,11... | collective-permute-start | bytes 786440 | tf_op jit(solution)/shard_map/ppermute | solution.py:40
  25.9 0.7 %shard_map.79 = (bf16[4,128,128]{2,1,0:T(8,128)(2,1)S(1)}, bf16[4,128,128]{2,1,0:T(8,128)(2,1)S(1)}) custom-call(bf16[2,640,1024]{2,1,0:T(8,128)(2,1)S(1)} %get-tuple-element.47.ds_ref.refs_4_, bf16[2,256,1024]{2,1,0:T(8,128)(2,1)S(1)} %get-tuple-element.52.p_ref, bf16[4,1024,128]{2,1,0:T(8,128)(2,1)S(1)} %get-tuple-element.40.refs_3_.qr_ref.refs_12_, ...), custom_call_target="tpu_custom_call" | custom-call | flops 134217728 | bytes 1048576 | tf_op jit(solution)/shard_map/pallas_call | solution.py:52
  26.6 0.2 collective-permute-done.6
  26.8 0.1 add_convert_fusion.2
  26.9 0.3 collective-permute-done.5.refs_2_.refs_8_
  27.2 3.9 %shard_map.80 = (bf16[8,128,128]{2,1,0:T(8,128)(2,1)S(1)}, bf16[2,640,1024]{2,1,0:T(8,128)(2,1)S(1)}, bf16[2,128,1024]{2,1,0:T(8,128)(2,1)S(1)}, bf16[2,256,1024]{2,1,0:T(8,128)(2,1)S(1)}) custom-call(bf16[4,128,128]{2,1,0:T(8,128)(2,1)S(1)} %collective-permute-done.3.refs_0_.refs_6_, bf16[4,128,128]{2,1,0:T(8,128)(2,1)S(1)} %collective-permute-done.4.refs_1_.refs_7_, ...), custom_call_target="tpu_custom_call" | custom-call | flops 1073741824 | bytes 1048576 | tf_op jit(solution)/shard_map/pallas_call | solution.py:52
  31.1 0.3 collective-permute-start.7
  31.4 0.5 %collective-permute-start.8 = (bf16[4,128,128]{2,1,0:T(8,128)(2,1)S(1)}, bf16[4,128,128]{2,1,0:T(8,128)(2,1)S(1)}, u32[]{:S(2)}, u32[]{:S(2)}) collective-permute-start(bf16[4,128,128]{2,1,0:T(8,128)(2,1)S(1)} %get-tuple-element.67), channel_id=1, source_target_pairs={{0,28},{1,29},{2,30},{3,31},{4,0},{5,1},{6,2},{7,3},{8,4},{9,5},{1... | collective-permute-start | bytes 393224 | tf_op jit(solution)/shard_map/ppermute | solution.py:29
  31.9 0.6 %collective-permute-start.9 = (bf16[4,128,128]{2,1,0:T(8,128)(2,1)S(1)}, bf16[4,128,128]{2,1,0:T(8,128)(2,1)S(1)}, u32[]{:S(2)}, u32[]{:S(2)}) collective-permute-start(bf16[4,128,128]{2,1,0:T(8,128)(2,1)S(1)} %get-tuple-element.68), channel_id=1, source_target_pairs={{0,30},{1,31},{2,0},{3,1},{4,2},{5,3},{6,4},{7,5},{8,6},{9,7},{10,... | collective-permute-start | bytes 393224 | tf_op jit(solution)/shard_map/ppermute | solution.py:29
  32.5 0.7 %shard_map.81 = (bf16[4,128,128]{2,1,0:T(8,128)(2,1)S(1)}, bf16[4,128,128]{2,1,0:T(8,128)(2,1)S(1)}) custom-call(bf16[2,640,1024]{2,1,0:T(8,128)(2,1)S(1)} %get-tuple-element.63.ds_ref.refs_10_, bf16[2,256,1024]{2,1,0:T(8,128)(2,1)S(1)} %get-tuple-element.58.p_ref, bf16[4,1024,128]{2,1,0:T(8,128)(2,1)S(1)} %get-tuple-element.40.refs_3_.qr_ref.refs_12_, ...), custom_call_target="tpu_custom_call" | custom-call | flops 134217728 | bytes 1048576 | tf_op jit(solution)/shard_map/pallas_call | solution.py:52
  33.3 0.0 collective-permute-done.7
  33.3 0.1 add_convert_fusion
  33.4 1.5 %collective-permute-start.10 = (bf16[4,128,128]{2,1,0:T(8,128)(2,1)S(1)}, bf16[4,128,128]{2,1,0:T(8,128)(2,1)S(1)}, u32[]{:S(2)}, u32[]{:S(2)}) collective-permute-start(bf16[4,128,128]{2,1,0:T(8,128)(2,1)S(1)} %get-tuple-element.69), channel_id=1, source_target_pairs={{0,28},{1,29},{2,30},{3,31},{4,0},{5,1},{6,2},{7,3},{8,4},{9,5},{1... | collective-permute-start | bytes 393224 | tf_op jit(solution)/shard_map/ppermute | solution.py:29
  34.8 1.5 %collective-permute-start.11 = (bf16[4,128,128]{2,1,0:T(8,128)(2,1)S(1)}, bf16[4,128,128]{2,1,0:T(8,128)(2,1)S(1)}, u32[]{:S(2)}, u32[]{:S(2)}) collective-permute-start(bf16[4,128,128]{2,1,0:T(8,128)(2,1)S(1)} %get-tuple-element.70), channel_id=1, source_target_pairs={{0,30},{1,31},{2,0},{3,1},{4,2},{5,3},{6,4},{7,5},{8,6},{9,7},{10,... | collective-permute-start | bytes 393224 | tf_op jit(solution)/shard_map/ppermute | solution.py:29
  36.4 2.6 %shard_map.82 = (bf16[128,32,128]{2,1,0:T(8,128)(2,1)}, f32[8,128,128]{2,1,0:T(8,128)S(1)}) custom-call(bf16[4,128,128]{2,1,0:T(8,128)(2,1)S(1)} %collective-permute-done.refs_0_, bf16[4,128,128]{2,1,0:T(8,128)(2,1)S(1)} %collective-permute-done.1.refs_1_, bf16[8,128,128]{2,1,0:T(8,128)(2,1)S(1)} %collective-permute-done.2.refs_2_, ...), custom_call_target="tpu_custom_call" | custom-call | flops 939524096 | bytes 1048576 | tf_op jit(solution)/shard_map/pallas_call | solution.py:52
  39.0 4.5 %collective-permute-done.8.refs_1_ = bf16[4,128,128]{2,1,0:T(8,128)(2,1)S(1)} collective-permute-done((bf16[4,128,128]{2,1,0:T(8,128)(2,1)S(1)}, bf16[4,128,128]{2,1,0:T(8,128)(2,1)S(1)}, u32[]{:S(2)}, u32[]{:S(2)}) %collective-permute-start.8) | collective-permute-done | bytes 131104 | tf_op jit(solution)/shard_map/ppermute | solution.py:29
  43.4 2.1 %collective-permute-done.10.refs_4_ = bf16[4,128,128]{2,1,0:T(8,128)(2,1)S(1)} collective-permute-done((bf16[4,128,128]{2,1,0:T(8,128)(2,1)S(1)}, bf16[4,128,128]{2,1,0:T(8,128)(2,1)S(1)}, u32[]{:S(2)}, u32[]{:S(2)}) %collective-permute-start.10) | collective-permute-done | bytes 131104 | tf_op jit(solution)/shard_map/ppermute | solution.py:29
  45.5 0.8 %shard_map.83 = (bf16[512,128]{1,0:T(8,128)(2,1)}, bf16[512,128]{1,0:T(8,128)(2,1)}) custom-call(f32[8,128,128]{2,1,0:T(8,128)S(1)} %get-tuple-element.66.own_ref, bf16[4,128,128]{2,1,0:T(8,128)(2,1)S(1)} %broadcast_select_fusion.1.refs_0_, bf16[4,128,128]{2,1,0:T(8,128)(2,1)S(1)} %collective-permute-done.8.refs_1_, ...), custom_call_target="tpu_custom_call" | custom-call | bytes 1048576 | tf_op jit(solution)/shard_map/pallas_call | solution.py:52
  (10 shorter events, 0.1 us)
Async XLA Ops:
  1.7 9.1 %collective-permute-start = (bf16[4,128,128]{2,1,0:T(8,128)(2,1)S(1)}, bf16[4,128,128]{2,1,0:T(8,128)(2,1)S(1)}, u32[]{:S(2)}, u32[]{:S(2)}) collective-permute-start(bf16[4,128,128]{2,1,0:T(8,128)(2,1)S(1)} %get-tuple-element.38.refs_0_.refs_3_), channel_id=1, source_target_pairs={{0,4},{1,5},{2,6},{3,7},{4,8},{5,9},{6,10},{7,11},{8,12},{9,13},{1... | collective-permute-start | bytes 393224 | tf_op jit(solution)/shard_map/ppermute | solution.py:29
  3.2 7.6 %collective-permute-start.1 = (bf16[4,128,128]{2,1,0:T(8,128)(2,1)S(1)}, bf16[4,128,128]{2,1,0:T(8,128)(2,1)S(1)}, u32[]{:S(2)}, u32[]{:S(2)}) collective-permute-start(bf16[4,128,128]{2,1,0:T(8,128)(2,1)S(1)} %get-tuple-element.38.refs_0_.refs_3_), channel_id=1, source_target_pairs={{0,2},{1,3},{2,4},{3,5},{4,6},{5,7},{6,8},{7,9},{8,10},{9,11},{10,... | collective-permute-start | bytes 393224 | tf_op jit(solution)/shard_map/ppermute | solution.py:29
  10.8 7.3 %collective-permute-start.2 = (bf16[8,128,128]{2,1,0:T(8,128)(2,1)S(1)}, bf16[8,128,128]{2,1,0:T(8,128)(2,1)S(1)}, u32[]{:S(2)}, u32[]{:S(2)}) collective-permute-start(bf16[8,128,128]{2,1,0:T(8,128)(2,1)S(1)} %pad_maximum_fusion), channel_id=1, source_target_pairs={{0,1},{1,0},{2,3},{3,2},{4,5},{5,4},{6,7},{7,6},{8,9},{9,8},{10,11... | collective-permute-start | bytes 786440 | tf_op jit(solution)/shard_map/ppermute | solution.py:40
  10.9 11.1 %collective-permute-start.4 = (bf16[4,128,128]{2,1,0:T(8,128)(2,1)S(1)}, bf16[4,128,128]{2,1,0:T(8,128)(2,1)S(1)}, u32[]{:S(2)}, u32[]{:S(2)}) collective-permute-start(bf16[4,128,128]{2,1,0:T(8,128)(2,1)S(1)} %get-tuple-element.39.refs_1_.refs_9_), channel_id=1, source_target_pairs={{0,2},{1,3},{2,4},{3,5},{4,6},{5,7},{6,8},{7,9},{8,10},{9,11},{10,... | collective-permute-start | bytes 393224 | tf_op jit(solution)/shard_map/ppermute | solution.py:29
  11.4 13.8 %collective-permute-start.3 = (bf16[4,128,128]{2,1,0:T(8,128)(2,1)S(1)}, bf16[4,128,128]{2,1,0:T(8,128)(2,1)S(1)}, u32[]{:S(2)}, u32[]{:S(2)}) collective-permute-start(bf16[4,128,128]{2,1,0:T(8,128)(2,1)S(1)} %get-tuple-element.39.refs_1_.refs_9_), channel_id=1, source_target_pairs={{0,4},{1,5},{2,6},{3,7},{4,8},{5,9},{6,10},{7,11},{8,12},{9,13},{1... | collective-permute-start | bytes 393224 | tf_op jit(solution)/shard_map/ppermute | solution.py:29
  14.8 0.7 %copy-start = (s32[3,128]{1,0:T(4,128)S(1)}, s32[3,128]{1,0:T(4,128)}, u32[]{:S(2)}) copy-start(s32[3,128]{1,0:T(4,128)} %bounds_ref.1) | copy-start | bytes 4612
  25.3 1.5 %collective-permute-start.6 = (bf16[8,128,128]{2,1,0:T(8,128)(2,1)S(1)}, bf16[8,128,128]{2,1,0:T(8,128)(2,1)S(1)}, u32[]{:S(2)}, u32[]{:S(2)}) collective-permute-start(bf16[8,128,128]{2,1,0:T(8,128)(2,1)S(1)} %get-tuple-element.54), channel_id=1, source_target_pairs={{0,1},{1,0},{2,3},{3,2},{4,5},{5,4},{6,7},{7,6},{8,9},{9,8},{10,11... | collective-permute-start | bytes 786440 | tf_op jit(solution)/shard_map/ppermute | solution.py:40
  25.3 1.9 %collective-permute-start.5 = (bf16[8,128,128]{2,1,0:T(8,128)(2,1)S(1)}, bf16[8,128,128]{2,1,0:T(8,128)(2,1)S(1)}, u32[]{:S(2)}, u32[]{:S(2)}) collective-permute-start(bf16[8,128,128]{2,1,0:T(8,128)(2,1)S(1)} %pad_maximum_fusion.1), channel_id=1, source_target_pairs={{0,1},{1,0},{2,3},{3,2},{4,5},{5,4},{6,7},{7,6},{8,9},{9,8},{10,11... | collective-permute-start | bytes 786440 | tf_op jit(solution)/shard_map/ppermute | solution.py:40
  31.1 2.2 %collective-permute-start.7 = (bf16[8,128,128]{2,1,0:T(8,128)(2,1)S(1)}, bf16[8,128,128]{2,1,0:T(8,128)(2,1)S(1)}, u32[]{:S(2)}, u32[]{:S(2)}) collective-permute-start(bf16[8,128,128]{2,1,0:T(8,128)(2,1)S(1)} %get-tuple-element.60), channel_id=1, source_target_pairs={{0,1},{1,0},{2,3},{3,2},{4,5},{5,4},{6,7},{7,6},{8,9},{9,8},{10,11... | collective-permute-start | bytes 786440 | tf_op jit(solution)/shard_map/ppermute | solution.py:40
  31.4 12.0 %collective-permute-start.8 = (bf16[4,128,128]{2,1,0:T(8,128)(2,1)S(1)}, bf16[4,128,128]{2,1,0:T(8,128)(2,1)S(1)}, u32[]{:S(2)}, u32[]{:S(2)}) collective-permute-start(bf16[4,128,128]{2,1,0:T(8,128)(2,1)S(1)} %get-tuple-element.67), channel_id=1, source_target_pairs={{0,28},{1,29},{2,30},{3,31},{4,0},{5,1},{6,2},{7,3},{8,4},{9,5},{1... | collective-permute-start | bytes 393224 | tf_op jit(solution)/shard_map/ppermute | solution.py:29
  31.9 11.5 %collective-permute-start.9 = (bf16[4,128,128]{2,1,0:T(8,128)(2,1)S(1)}, bf16[4,128,128]{2,1,0:T(8,128)(2,1)S(1)}, u32[]{:S(2)}, u32[]{:S(2)}) collective-permute-start(bf16[4,128,128]{2,1,0:T(8,128)(2,1)S(1)} %get-tuple-element.68), channel_id=1, source_target_pairs={{0,30},{1,31},{2,0},{3,1},{4,2},{5,3},{6,4},{7,5},{8,6},{9,7},{10,... | collective-permute-start | bytes 393224 | tf_op jit(solution)/shard_map/ppermute | solution.py:29
  33.4 12.1 %collective-permute-start.10 = (bf16[4,128,128]{2,1,0:T(8,128)(2,1)S(1)}, bf16[4,128,128]{2,1,0:T(8,128)(2,1)S(1)}, u32[]{:S(2)}, u32[]{:S(2)}) collective-permute-start(bf16[4,128,128]{2,1,0:T(8,128)(2,1)S(1)} %get-tuple-element.69), channel_id=1, source_target_pairs={{0,28},{1,29},{2,30},{3,31},{4,0},{5,1},{6,2},{7,3},{8,4},{9,5},{1... | collective-permute-start | bytes 393224 | tf_op jit(solution)/shard_map/ppermute | solution.py:29
  34.8 10.7 %collective-permute-start.11 = (bf16[4,128,128]{2,1,0:T(8,128)(2,1)S(1)}, bf16[4,128,128]{2,1,0:T(8,128)(2,1)S(1)}, u32[]{:S(2)}, u32[]{:S(2)}) collective-permute-start(bf16[4,128,128]{2,1,0:T(8,128)(2,1)S(1)} %get-tuple-element.70), channel_id=1, source_target_pairs={{0,30},{1,31},{2,0},{3,1},{4,2},{5,3},{6,4},{7,5},{8,6},{9,7},{10,... | collective-permute-start | bytes 393224 | tf_op jit(solution)/shard_map/ppermute | solution.py:29
